TPU v7x, 32 devices: a whole 2x2x4 slice. The times are simulated.
32 devices in a mesh: dp: 4 (over z), row: 4 (over x, core), col: 2 (over y).
Axes of the slice: x: 2, y: 2, z: 4, core: 2. Of those that a mesh axis runs over, the one named last changes fastest.
Arguments:
- block_input: float32 [23328, 1152], P(('dp', 'row'), 'col'), may hold values from -32 to 32
- qkv_weight: bfloat16 [3, 1152, 1152], P(None, 'col', 'row'), may hold values from -0.1875 to 0.1875
- query_bias: float32 [1152], P('row'), may hold values from -3 to 3
- value_bias: float32 [1152], P('row'), may hold values from -3 to 3
- out_weight: bfloat16 [1152, 1152], P('row', 'col'), may hold values from -0.75 to 0.75
- out_bias: float32 [1152], P('col'), may hold values from -2 to 2
- first_gain: float32 [1152], P('col'), may hold values from 0.3 to 2.4
- first_shift: float32 [1152], P('col'), may hold values from -2 to 2
- second_gain: float32 [1152], P('col'), may hold values from 0.3 to 2.4
- second_shift: float32 [1152], P('col'), may hold values from -2 to 2
- up_weight: bfloat16 [1152, 4304], P('col', 'row'), may hold values from -0.1875 to 0.1875
- up_bias: float32 [4304], P('row'), may hold values from -3 to 3
- down_weight: bfloat16 [4304, 1152], P('row', 'col'), may hold values from -0.09375 to 0.09375
- down_bias: float32 [1152], P('col'), may hold values from -3 to 3
- out_cotangent: float32 [23328, 1152], P(('dp', 'row'), 'col'), may hold values from -6 to 6
Outputs:
- block_output: float32 [23328, 1152], P(('dp', 'row'), 'col')
- input_grad: float32 [23328, 1152], P(('dp', 'row'), 'col')
- qkv_grad: float32 [3, 1152, 1152], P(None, 'col', 'row')
- query_bias_grad: float32 [1152], P('row')
- value_bias_grad: float32 [1152], P('row')
- out_weight_grad: float32 [1152, 1152], P('row', 'col')
- out_bias_grad: float32 [1152], P('col')
- first_gain_grad: float32 [1152], P('col')
- first_shift_grad: float32 [1152], P('col')
- second_gain_grad: float32 [1152], P('col')
- second_shift_grad: float32 [1152], P('col')
- up_weight_grad: float32 [1152, 4304], P('col', 'row')
- up_bias_grad: float32 [4304], P('row')
- down_weight_grad: float32 [4304, 1152], P('row', 'col')
- down_bias_grad: float32 [1152], P('col')
All inputs are finite; a program needn't handle non-finite values.
Results may differ from a plain program's by a relative error of at most 0.03.
Values may be sent and summed in bfloat16 or wider, within the bound.
No kernel may reach another device: no remote copies, remote signals or barrier semaphores. Data moves between devices by JAX's collectives and lax.ppermute only.
A program may use at most 320 MiB of HBM per device.

v0:
```python
import jax
import jax.numpy as jnp
from jax import lax
from jax.sharding import PartitionSpec as P

HD = 72
S = 729
IMG_DEV = 8
EPSILON = 1e-06


def gelu_tanh(tensor):
    return jax.nn.gelu(tensor, approximate=True)


def times_weight(weight_block):

    def apply_rows(row_block):
        return jnp.dot(row_block, weight_block, preferred_element_type=jnp.float32)

    return apply_rows


def times_transpose(weight_block):

    def apply_rows(row_block):
        return lax.dot_general(
            row_block, weight_block, (((1,), (1,)), ((), ())), preferred_element_type=jnp.float32
        )

    return apply_rows


def contract_rows(left, right):
    return lax.dot_general(
        left, right, (((0,), (0,)), ((), ())), preferred_element_type=jnp.float32
    )


def local_norm(values, norm_gain, norm_shift):
    width = values.shape[1] * lax.axis_size("col")
    totals, squares = lax.psum((jnp.sum(values, axis=1), jnp.sum(values * values, axis=1)), "col")
    mean_val = totals / width
    var_val = squares / width - mean_val * mean_val
    centered = values - mean_val[:, None]
    inv_dev = lax.rsqrt(var_val + EPSILON)[:, None]
    normed = centered * inv_dev
    return ((normed * norm_gain + norm_shift).astype(jnp.bfloat16), normed, inv_dev)


def local_norm_back(grad_out, normed, inv_dev, norm_gain):
    width = grad_out.shape[1] * lax.axis_size("col")
    scaled = grad_out * norm_gain
    first_sum, second_sum = lax.psum(
        (jnp.sum(scaled, axis=1), jnp.sum(scaled * normed, axis=1)), "col"
    )
    return inv_dev * (scaled - first_sum[:, None] / width - normed * (second_sum[:, None] / width))


def rows_then_width(local_rows, weight_fn):
    gathered = lax.all_gather(local_rows, "row", axis=0, tiled=True)
    return (
        gathered,
        lax.psum_scatter(
            weight_fn(gathered).astype(jnp.bfloat16), "col", scatter_dimension=0, tiled=True
        ).astype(jnp.float32),
    )


def halves_then_heads(local_rows, weight_fn):
    gathered = lax.all_gather(local_rows, "col", axis=0, tiled=True)
    return (
        gathered,
        lax.psum_scatter(
            weight_fn(gathered).astype(jnp.bfloat16), "row", scatter_dimension=0, tiled=True
        ).astype(jnp.float32),
    )


def attend_local(query_rows, key_rows, value_rows):
    score_scale = HD ** (-0.5)

    def one_image(operands):
        query_img, key_img, value_img = operands
        scores = (
            jnp.einsum("shd,thd->hst", query_img, key_img, preferred_element_type=jnp.float32)
            * score_scale
        )
        row_top = jnp.max(scores, axis=-1, keepdims=True)
        logsum = row_top + jnp.log(jnp.sum(jnp.exp(scores - row_top), axis=-1, keepdims=True))
        soft_weights = jnp.exp(scores - logsum).astype(jnp.bfloat16)
        attended = jnp.einsum(
            "hst,thd->shd", soft_weights, value_img, preferred_element_type=jnp.float32
        )
        return (attended.astype(jnp.bfloat16), logsum)

    return lax.map(one_image, (query_rows, key_rows, value_rows))


def attend_local_back(query_rows, key_rows, value_rows, logsum, grad_attended):
    score_scale = HD ** (-0.5)

    def one_image(operands):
        query_img, key_img, value_img, logsum_img, grad_img = operands
        scores = (
            jnp.einsum("shd,thd->hst", query_img, key_img, preferred_element_type=jnp.float32)
            * score_scale
        )
        soft = jnp.exp(scores - logsum_img)
        grad_value = jnp.einsum(
            "hst,shd->thd", soft.astype(jnp.bfloat16), grad_img, preferred_element_type=jnp.float32
        )
        grad_soft = jnp.einsum(
            "shd,thd->hst", grad_img, value_img, preferred_element_type=jnp.float32
        )
        row_delta = jnp.sum(soft * grad_soft, axis=-1, keepdims=True)
        grad_scores = (soft * (grad_soft - row_delta)).astype(jnp.bfloat16)
        grad_query = (
            jnp.einsum("hst,thd->shd", grad_scores, key_img, preferred_element_type=jnp.float32)
            * score_scale
        )
        grad_key = (
            jnp.einsum("hst,shd->thd", grad_scores, query_img, preferred_element_type=jnp.float32)
            * score_scale
        )
        return (
            grad_query.astype(jnp.bfloat16),
            grad_key.astype(jnp.bfloat16),
            grad_value.astype(jnp.bfloat16),
        )

    return lax.map(one_image, (query_rows, key_rows, value_rows, logsum, grad_attended))


def grid_body(
    block_input,
    qkv_weight,
    query_bias,
    value_bias,
    out_weight,
    out_bias,
    first_gain,
    first_shift,
    second_gain,
    second_shift,
    up_weight,
    up_bias,
    down_weight,
    down_bias,
    out_cotangent,
):
    images_all = IMG_DEV * lax.axis_size("dp")
    width_cols = qkv_weight.shape[1]
    head_cols = qkv_weight.shape[2]
    local_heads = head_cols // HD
    flat_qkv = jnp.transpose(qkv_weight, (1, 0, 2)).reshape(width_cols, 3 * head_cols)
    first_normed, first_hat, first_inv = local_norm(block_input, first_gain, first_shift)
    first_gathered, qkv_part = rows_then_width(first_normed, times_weight(flat_qkv))
    rows_half = qkv_part.shape[0]
    image_count = rows_half // S
    head_shape = (image_count, S, local_heads, HD)
    qkv_part = qkv_part.reshape(rows_half, 3, head_cols)
    query_rows = (qkv_part[:, 0] + query_bias).astype(jnp.bfloat16).reshape(head_shape)
    key_rows = qkv_part[:, 1].astype(jnp.bfloat16).reshape(head_shape)
    value_rows = (qkv_part[:, 2] + value_bias).astype(jnp.bfloat16).reshape(head_shape)
    attended, logsum = attend_local(query_rows, key_rows, value_rows)
    attended_flat = attended.reshape(rows_half, head_cols)
    attended_gathered, attn_proj = halves_then_heads(attended_flat, times_weight(out_weight))
    middle = block_input + attn_proj + out_bias
    second_normed, second_hat, second_inv = local_norm(middle, second_gain, second_shift)
    second_gathered, pre_act = rows_then_width(second_normed, times_weight(up_weight))
    pre_act = pre_act + up_bias
    hidden = gelu_tanh(pre_act).astype(jnp.bfloat16)
    hidden_gathered, mlp_proj = halves_then_heads(hidden, times_weight(down_weight))
    block_output = middle + mlp_proj + down_bias
    cot_rounded = out_cotangent.astype(jnp.bfloat16)
    cot_gathered, grad_hidden = rows_then_width(cot_rounded, times_transpose(down_weight))
    down_w_grad = contract_rows(hidden_gathered, cot_gathered) / images_all
    down_b_grad = jnp.sum(cot_gathered, axis=0, dtype=jnp.float32) / images_all
    grad_pre = jax.vjp(gelu_tanh, pre_act)[1](grad_hidden)[0].astype(jnp.bfloat16)
    pre_gathered, grad_second = halves_then_heads(grad_pre, times_transpose(up_weight))
    up_w_grad = contract_rows(second_gathered, pre_gathered) / images_all
    up_b_grad = jnp.sum(pre_gathered, axis=0, dtype=jnp.float32) / images_all
    second_gain_part = jnp.sum(grad_second * second_hat, axis=0) / images_all
    second_shift_part = jnp.sum(grad_second, axis=0) / images_all
    grad_middle = out_cotangent + local_norm_back(grad_second, second_hat, second_inv, second_gain)
    middle_rounded = grad_middle.astype(jnp.bfloat16)
    middle_gathered, grad_attended = rows_then_width(middle_rounded, times_transpose(out_weight))
    out_w_grad = contract_rows(attended_gathered, middle_gathered) / images_all
    out_b_grad = jnp.sum(middle_gathered, axis=0, dtype=jnp.float32) / images_all
    grad_attended = grad_attended.astype(jnp.bfloat16).reshape(head_shape)
    grad_query, grad_key, grad_value = attend_local_back(
        query_rows, key_rows, value_rows, logsum, grad_attended
    )
    grad_qkv = jnp.stack(
        [
            grad_query.reshape(rows_half, head_cols),
            grad_key.reshape(rows_half, head_cols),
            grad_value.reshape(rows_half, head_cols),
        ],
        axis=1,
    ).reshape(rows_half, 3 * head_cols)
    qkv_gathered, grad_first = halves_then_heads(grad_qkv, times_transpose(flat_qkv))
    qkv_w_grad = (
        (contract_rows(first_gathered, qkv_gathered) / images_all)
        .reshape(width_cols, 3, head_cols)
        .transpose(1, 0, 2)
    )
    query_b_grad = jnp.sum(qkv_gathered[:, :head_cols], axis=0, dtype=jnp.float32) / images_all
    value_b_grad = jnp.sum(qkv_gathered[:, 2 * head_cols :], axis=0, dtype=jnp.float32) / images_all
    (
        qkv_w_grad,
        query_b_grad,
        value_b_grad,
        out_w_grad,
        out_b_grad,
        up_w_grad,
        up_b_grad,
        down_w_grad,
        down_b_grad,
    ) = (
        lax.psum(qkv_w_grad.astype(jnp.bfloat16), "dp").astype(jnp.float32),
        lax.psum(query_b_grad.astype(jnp.bfloat16), "dp").astype(jnp.float32),
        lax.psum(value_b_grad.astype(jnp.bfloat16), "dp").astype(jnp.float32),
        lax.psum(out_w_grad.astype(jnp.bfloat16), "dp").astype(jnp.float32),
        lax.psum(out_b_grad.astype(jnp.bfloat16), "dp").astype(jnp.float32),
        lax.psum(up_w_grad.astype(jnp.bfloat16), "dp").astype(jnp.float32),
        lax.psum(up_b_grad.astype(jnp.bfloat16), "dp").astype(jnp.float32),
        lax.psum(down_w_grad.astype(jnp.bfloat16), "dp").astype(jnp.float32),
        lax.psum(down_b_grad.astype(jnp.bfloat16), "dp").astype(jnp.float32),
    )
    first_gain_part = jnp.sum(grad_first * first_hat, axis=0) / images_all
    first_shift_part = jnp.sum(grad_first, axis=0) / images_all
    grad_input = grad_middle + local_norm_back(grad_first, first_hat, first_inv, first_gain)
    first_gain_grad, first_shift_grad, second_gain_grad, second_shift_grad = lax.psum(
        (first_gain_part, first_shift_part, second_gain_part, second_shift_part), ("dp", "row")
    )
    return (
        block_output,
        grad_input,
        qkv_w_grad,
        query_b_grad,
        value_b_grad,
        out_w_grad,
        out_b_grad,
        first_gain_grad,
        first_shift_grad,
        second_gain_grad,
        second_shift_grad,
        up_w_grad,
        up_b_grad,
        down_w_grad,
        down_b_grad,
    )


def shards(
    block_input,
    qkv_weight,
    query_bias,
    value_bias,
    out_weight,
    out_bias,
    first_gain,
    first_shift,
    second_gain,
    second_shift,
    up_weight,
    up_bias,
    down_weight,
    down_bias,
    out_cotangent,
):
    return grid_body(
        block_input,
        qkv_weight,
        query_bias,
        value_bias,
        out_weight,
        out_bias,
        first_gain,
        first_shift,
        second_gain,
        second_shift,
        up_weight,
        up_bias,
        down_weight,
        down_bias,
        out_cotangent,
    )


def solution(mesh):
    return jax.shard_map(
        shards,
        mesh=mesh,
        in_specs=(
            P(("dp", "row"), "col"),
            P(None, "col", "row"),
            P("row"),
            P("row"),
            P("row", "col"),
            P("col"),
            P("col"),
            P("col"),
            P("col"),
            P("col"),
            P("col", "row"),
            P("row"),
            P("row", "col"),
            P("col"),
            P(("dp", "row"), "col"),
        ),
        out_specs=(
            P(("dp", "row"), "col"),
            P(("dp", "row"), "col"),
            P(None, "col", "row"),
            P("row"),
            P("row"),
            P("row", "col"),
            P("col"),
            P("col"),
            P("col"),
            P("col"),
            P("col"),
            P("col", "row"),
            P("row"),
            P("row", "col"),
            P("col"),
        ),
        check_vma=False,
    )
```

profile of v0, /device:TPU:0, one launch (start us, length us, event | category | flops | bytes accessed | tf_op | source)
XLA Modules:
  0.0 2734.9 jit_solution(11299218937479715153)
XLA Ops:
  24.0 51.2 %all-gather.17.cloned.1.call-done = bf16[4,1458,576]{1,2,0:T(8,128)(2,1)} async-done(((bf16[1,1458,576]{1,2,0:T(8,128)(2,1)}), bf16[4,1458,576]{1,2,0:T(8,128)(2,1)}) %all-gather.17.cloned.1.call-update) | async-done | bytes 6718480 | tf_op jit(solution)/shard_map/all_gather | solution.py:61
  75.2 11.3 copy.64
  86.5 12.7 reshape.122
  99.2 13.1 convolution_convert_fusion.2
  114.4 234.6 %all-reduce.25.cloned.1.call-done = bf16[5832,864]{0,1:T(8,128)(2,1)} async-done(((bf16[5832,864]{0,1:T(8,128)(2,1)}), bf16[5832,864]{0,1:T(8,128)(2,1)}) %all-reduce.25.cloned.1.call-update) | async-done | bytes 10077712
  384.8 29.9 %while.26 = (s32[]{:T(128)}, bf16[4,729,4,72]{1,3,2,0:T(8,128)(2,1)}, f32[4,4,729,1]{2,1,3,0:T(4,128)S(1)}, bf16[4,729,4,72]{1,3,2,0:T(8,128)(2,1)}, bf16[4,729,...) while((s32[]{:T(128)}, bf16[4,729,4,72]{1,3,2,0:T(8,128)(2,1)}, ...), condition=%wide.region_8.9_spmd, body=%wide.region_5.8_spmd.sunk | while | flops 629433152 | bytes 27376584 | solution.py:97
  418.7 15.4 reshape.123
  434.2 47.8 %all-gather.19.cloned.1.call-done = bf16[2,2916,288]{1,2,0:T(8,128)(2,1)} async-done(((bf16[1,2916,288]{1,2,0:T(8,128)(2,1)}), bf16[2,2916,288]{1,2,0:T(8,128)(2,1)}) %all-gather.19.cloned.1.call-update) | async-done | bytes 3359248 | tf_op jit(solution)/shard_map/all_gather | solution.py:71
  508.0 122.8 %all-reduce.27.cloned.1.call-done = bf16[5832,576]{0,1:T(8,128)(2,1)} async-done(((bf16[5832,576]{0,1:T(8,128)(2,1)}), bf16[5832,576]{0,1:T(8,128)(2,1)}) %all-reduce.27.cloned.1.call-update) | async-done | bytes 6718480
  648.5 34.8 %all-gather.25.cloned.1.call-done = bf16[4,1458,576]{1,2,0:T(8,128)(2,1)} async-done(((bf16[1,1458,576]{1,2,0:T(8,128)(2,1)}), bf16[4,1458,576]{1,2,0:T(8,128)(2,1)}) %all-gather.25.cloned.1.call-update) | async-done | bytes 6718480 | tf_op jit(solution)/shard_map/all_gather | solution.py:61
  683.4 11.9 copy.72
  695.3 13.2 reshape.130
  708.5 15.8 convolution_convert_fusion
  724.2 12.0 all-gather.21.cloned.1.call-done
  736.2 11.4 copy.70
  747.6 12.6 reshape.126
  760.2 16.1 convolution_convert_fusion.1
  776.3 563.8 %all-reduce.37.cloned.1.call-done = (bf16[5832,1076]{0,1:T(8,128)(2,1)}, bf16[5832,1076]{0,1:T(8,128)(2,1)}) async-done(((bf16[5832,1076]{0,1:T(8,128)(2,1)}, bf16[5832,1076]{0,1:T(8,128)(2,1)}), (bf16[5832,1076]{0,1:T(8,128)(2,1)}, bf16[5832,1076]{0,1:T(8,128)(2,1)})) %all-reduce.37.cloned.1.call-update) | async-done | bytes 25100944
  1340.1 20.3 fusion.71
  1360.5 154.6 %all-gather.27.cloned.1.call-done = bf16[2,2916,1076]{1,2,0:T(8,128)(2,1)} async-done(((bf16[1,2916,1076]{1,2,0:T(8,128)(2,1)}), bf16[2,2916,1076]{1,2,0:T(8,128)(2,1)}) %all-gather.27.cloned.1.call-update) | async-done | bytes 12550480 | tf_op jit(solution)/shard_map/all_gather | solution.py:71
  1515.1 48.6 %copy.73 = bf16[2,2916,1076]{1,0,2:T(2,128)(2,1)} copy(bf16[2,2916,1076]{1,2,0:T(8,128)(2,1)} %all-gather.27.cloned.1.call-done) | data formatting | bytes 25100928 | tf_op jit(solution)/shard_map/all_gather | solution.py:71
  1563.7 25.6 reshape.132
  1589.3 15.3 convolution_convert_fusion.3
  1604.7 127.7 %all-reduce.29.cloned.1.call-done = bf16[5832,576]{0,1:T(8,128)(2,1)} async-done(((bf16[5832,576]{0,1:T(8,128)(2,1)}), bf16[5832,576]{0,1:T(8,128)(2,1)}) %all-reduce.29.cloned.1.call-update) | async-done | bytes 6718480
  1753.2 49.8 %all-gather.29.cloned.1.call-done = bf16[4,1458,576]{1,2,0:T(8,128)(2,1)} async-done(((bf16[1,1458,576]{1,2,0:T(8,128)(2,1)}), bf16[4,1458,576]{1,2,0:T(8,128)(2,1)}) %all-gather.29.cloned.1.call-update) | async-done | bytes 6718480 | tf_op jit(solution)/shard_map/all_gather | solution.py:61
  1803.1 11.3 copy.74
  1814.4 12.6 reshape.134
  1834.9 90.5 %all-reduce.31.cloned.1.call-done = bf16[5832,288]{0,1:T(8,128)(2,1)} async-done(((bf16[5832,288]{0,1:T(8,128)(2,1)}), bf16[5832,288]{0,1:T(8,128)(2,1)}) %all-reduce.31.cloned.1.call-update) | async-done | bytes 3359248
  1941.6 118.4 %while.27 = (s32[]{:T(128)}, bf16[4,729,4,72]{1,3,2,0:T(8,128)(2,1)}, bf16[4,729,4,72]{1,3,2,0:T(8,128)(2,1)}, bf16[4,729,4,72]{1,3,2,0:T(8,128)(2,1)}, bf16[4,7...) while((s32[]{:T(128)}, ...), condition=%wide.region_25.26_spmd, body=%wide.region_23.25_spmd.sunk | while | flops 1557106048 | bytes 127373888 | solution.py:132
  1954.1 10.3 multiply_convert_fusion.9
  1983.5 10.3 multiply_convert_fusion.9
  2012.9 10.3 multiply_convert_fusion.9
  2042.4 10.3 multiply_convert_fusion.9
  2086.5 48.3 %copy.71 = bf16[2,2916,1076]{1,0,2:T(2,128)(2,1)} copy(bf16[2,2916,1076]{1,2,0:T(8,128)(2,1)} %all-gather.23.cloned.1.call-done) | data formatting | bytes 25100928 | tf_op jit(solution)/shard_map/all_gather | solution.py:71
  2134.8 25.6 reshape.128
  2160.5 14.6 fusion.89
  2175.1 14.8 fusion.88
  2193.5 19.3 all-gather.31.cloned.1.call-done
  2212.8 13.7 copy.82
  2226.5 14.0 reshape.136
  2240.5 12.3 multiply_convert_fusion.2
  2254.4 15.5 convolution_convert_fusion.4
  2269.9 12.2 convolution_convert_fusion.5
  2303.8 20.4 all-reduce.14
  2327.1 80.7 %all-reduce.35.cloned.1.call-done = (bf16[3,576,288]{1,2,0:T(8,128)(2,1)}, bf16[288,576]{1,0:T(8,128)(2,1)}, bf16[576,1076]{1,0:T(8,128)(2,1)}, bf16[1076,576]{0,1:T(8,128)(2,1)}) async-done(((bf16[3,576,288]{1,2,0:T(8,128)(2,1)}, bf16[288,576]{1,0:T(8,128)(2,1)}, bf16[576,1076]{1,0:T(8,128)(2,1)}, bf16[1076,576]{0,1:T(8,128)(2,1)}), (bf16[3,576,288]{1,2,0:T(8,128)(2,1)}, bf16[288,576]{1,0:T(8,128)(2,1)}, ...) | async-done | bytes 3806224 | tf_op jit(solution)/shard_map/psum | solution.py:222
  2416.1 229.7 %all-reduce.33.cloned.1.call-done = (bf16[5832,576]{0,1:T(8,128)(2,1)}, bf16[5832,576]{0,1:T(8,128)(2,1)}) async-done(((bf16[5832,576]{0,1:T(8,128)(2,1)}, bf16[5832,576]{0,1:T(8,128)(2,1)}), (bf16[5832,576]{0,1:T(8,128)(2,1)}, bf16[5832,576]{0,1:T(8,128)(2,1)})) %all-reduce.33.cloned.1.call-update) | async-done | bytes 13436944
  2659.0 58.9 %all-reduce.8 = (f32[576]{0:T(1024)}, f32[576]{0:T(1024)}, f32[576]{0:T(1024)}, f32[576]{0:T(1024)}) all-reduce(f32[576]{0:T(1024)S(1)} %broadcast_multiply_fusion.9, f32[576]{0:T(1024)S(1)} %broadcast_multiply_fusion.8, f32[576]{0:T(1024)S(1)} %get-tuple-element.228, ...), channel_id=1, replica_groups=mesh['dp'=4,'row'=4,'col'=2] {'dp','row'}, use_global_device_ids=true, to_apply=%region_40.41 | all-reduce | flops 2304 | bytes 18432 | tf_op jit(solution)/shard_map/psum | solution.py:235
  2717.9 9.9 fusion.80
  (251 shorter events, 330.6 us)
Async XLA Ops:
  7.2 753.0 %copy-start = (bf16[576,1076]{1,0:T(8,128)(2,1)S(1)}, bf16[576,1076]{1,0:T(8,128)(2,1)}, u32[]{:S(2)}) copy-start(bf16[576,1076]{1,0:T(8,128)(2,1)} %param.29) | copy-start | bytes 3718660
  7.2 12.9 copy-start.24
  7.2 12.9 copy-start.31
  7.2 67.9 %all-gather.17.cloned.1.call-start = ((), (), s32[]{:S(2)}) async-start(), calls=%async_computation | async-start | bytes 8847360 | tf_op jit(solution)/shard_map/all_gather | solution.py:61
  23.9 325.1 %all-reduce.25.cloned.1.call-start = ((), (), s32[]{:S(2)}) async-start(), calls=%async_computation.8 | async-start | bytes 20348928
  86.5 12.7 copy-start.36
  112.3 369.7 %all-gather.19.cloned.1.call-start = ((), (), s32[]{:S(2)}) async-start(), calls=%async_computation.1 | async-start | bytes 5087232 | tf_op jit(solution)/shard_map/all_gather | solution.py:71
  434.1 196.7 %all-reduce.27.cloned.1.call-start = ((), (), s32[]{:S(2)}) async-start(), calls=%async_computation.9 | async-start | bytes 13565952
  488.3 6.4 copy-start.38
  503.2 127.7 %copy-start.29 = (f32[576]{0:T(1024)S(1)}, f32[576]{0:T(1024)}, u32[]{:S(2)}) copy-start(f32[576]{0:T(1024)} %param.24) | copy-start | bytes 6916
  503.2 180.2 %all-gather.25.cloned.1.call-start = ((), (), s32[]{:S(2)}) async-start(), calls=%async_computation.4 | async-start | bytes 8847360 | tf_op jit(solution)/shard_map/all_gather | solution.py:61
  506.7 229.5 %all-gather.21.cloned.1.call-start = ((), (), s32[]{:S(2)}) async-start(), calls=%async_computation.2 | async-start | bytes 8847360 | tf_op jit(solution)/shard_map/all_gather | solution.py:61
  508.0 136.7 %copy-start.22 = (f32[576]{0:T(1024)S(1)}, f32[576]{0:T(1024)}, u32[]{:S(2)}) copy-start(f32[576]{0:T(1024)} %param.27) | copy-start | bytes 6916
  508.0 136.7 %copy-start.32 = (f32[576]{0:T(1024)S(1)}, f32[576]{0:T(1024)}, u32[]{:S(2)}) copy-start(f32[576]{0:T(1024)} %param.28) | copy-start | bytes 6916
  644.6 1101.4 %copy-start.10 = (f32[1458]{0:T(1024)}, f32[1458]{0:T(1024)S(1)}, u32[]{:S(2)}) copy-start(f32[1458]{0:T(1024)S(1)} %get-tuple-element.223) | copy-start | bytes 17500
  644.7 1101.4 %copy-start.12 = (f32[1458]{0:T(1024)}, f32[1458]{0:T(1024)S(1)}, u32[]{:S(2)}) copy-start(f32[1458]{0:T(1024)S(1)} %get-tuple-element.224) | copy-start | bytes 17500
  648.5 691.6 %all-reduce.37.cloned.1.call-start = ((), (), s32[]{:S(2)}) async-start(), calls=%async_computation.14 | async-start | bytes 50872320
  776.2 563.9 %copy-start.28 = (f32[1076]{0:T(1024)S(1)}, f32[1076]{0:T(1024)}, u32[]{:S(2)}) copy-start(f32[1076]{0:T(1024)} %param.30) | copy-start | bytes 12916
  776.3 738.9 %all-gather.27.cloned.1.call-start = ((), (), s32[]{:S(2)}) async-start(), calls=%async_computation.5 | async-start | bytes 19077120 | tf_op jit(solution)/shard_map/all_gather | solution.py:71
  1360.5 371.8 %all-reduce.29.cloned.1.call-start = ((), (), s32[]{:S(2)}) async-start(), calls=%async_computation.10 | async-start | bytes 13565952
  1604.6 198.5 %all-gather.29.cloned.1.call-start = ((), (), s32[]{:S(2)}) async-start(), calls=%async_computation.6 | async-start | bytes 8847360 | tf_op jit(solution)/shard_map/all_gather | solution.py:61
  1746.0 6.8 copy-start.18
  1746.0 6.8 copy-start.20
  1752.8 172.6 %all-reduce.31.cloned.1.call-start = ((), (), s32[]{:S(2)}) async-start(), calls=%async_computation.11 | async-start | bytes 6782976
  1834.1 252.4 %all-gather.23.cloned.1.call-start = ((), (), s32[]{:S(2)}) async-start(), calls=%async_computation.3 | async-start | bytes 19077120 | tf_op jit(solution)/shard_map/all_gather | solution.py:71
  1834.7 378.1 %all-gather.31.cloned.1.call-start = ((), (), s32[]{:S(2)}) async-start(), calls=%async_computation.7 | async-start | bytes 15261696 | tf_op jit(solution)/shard_map/all_gather | solution.py:71
  1993.7 4.7 copy-start.3
  2052.6 4.7 copy-start.3
  2065.8 8.6 copy-start.5
  2086.4 321.4 %all-reduce.35.cloned.1.call-start = ((), (), s32[]{:S(2)}) async-start(), calls=%async_computation.13 | async-start | bytes 8257536 | tf_op jit(solution)/shard_map/psum | solution.py:222
  2160.4 29.4 %slice-start = ((s8[6782976]{0:T(1024)(128)(4,1)}), s8[4194304]{0:T(1024)(128)(4,1)S(1)}, s32[]{:S(2)}) async-start(s8[6782976]{0:T(1024)(128)(4,1)} %bitcast.195), calls=%async_computation.15 | async-start | bytes 8388608
  2175.1 14.8 slice-start.1
  2175.1 14.8 copy-start.7
  2254.3 15.6 copy-start.37
  2254.3 391.5 %all-reduce.33.cloned.1.call-start = ((), (), s32[]{:S(2)}) async-start(), calls=%async_computation.12 | async-start | bytes 27131904
  2286.1 6.6 copy-start.26
  2286.1 6.6 copy-start.27
  2407.8 4.9 copy-start.9
  2412.7 233.1 %copy-start.15 = (f32[1458]{0:T(1024)S(1)}, f32[1458]{0:T(1024)}, u32[]{:S(2)}) copy-start(f32[1458]{0:T(1024)} %copy-done.14) | copy-start | bytes 17500
  2412.7 233.1 %copy-start.17 = (f32[1458]{0:T(1024)S(1)}, f32[1458]{0:T(1024)}, u32[]{:S(2)}) copy-start(f32[1458]{0:T(1024)} %copy-done.16) | copy-start | bytes 17500
  2412.7 233.1 %copy-start.25 = (f32[576]{0:T(1024)S(1)}, f32[576]{0:T(1024)}, u32[]{:S(2)}) copy-start(f32[576]{0:T(1024)} %param.25) | copy-start | bytes 6916
  2416.1 301.7 %copy-start.11 = (f32[1458]{0:T(1024)S(1)}, f32[1458]{0:T(1024)}, u32[]{:S(2)}) copy-start(f32[1458]{0:T(1024)} %copy-done.10) | copy-start | bytes 17500
  2416.1 301.7 %copy-start.13 = (f32[1458]{0:T(1024)S(1)}, f32[1458]{0:T(1024)}, u32[]{:S(2)}) copy-start(f32[1458]{0:T(1024)} %copy-done.12) | copy-start | bytes 17500
  2416.1 301.7 %copy-start.19 = (f32[1458]{0:T(1024)S(1)}, f32[1458]{0:T(1024)}, u32[]{:S(2)}) copy-start(f32[1458]{0:T(1024)} %copy-done.18) | copy-start | bytes 17500
  2416.1 301.8 %copy-start.21 = (f32[1458]{0:T(1024)S(1)}, f32[1458]{0:T(1024)}, u32[]{:S(2)}) copy-start(f32[1458]{0:T(1024)} %copy-done.20) | copy-start | bytes 17500
  2416.1 301.8 %copy-start.23 = (f32[576]{0:T(1024)S(1)}, f32[576]{0:T(1024)}, u32[]{:S(2)}) copy-start(f32[576]{0:T(1024)} %param.27) | copy-start | bytes 6916
  2416.1 301.8 %copy-start.30 = (f32[576]{0:T(1024)S(1)}, f32[576]{0:T(1024)}, u32[]{:S(2)}) copy-start(f32[576]{0:T(1024)} %param.32) | copy-start | bytes 6916
  2717.9 9.9 copy-start.1
  (19 other events, 52.1 us)
Sparse Core Ops, SparseCore 0:
  24.1 51.0 all-gather.16
  112.4 236.5 all-reduce.24
  434.3 47.6 all-gather.18
  503.3 127.5 all-reduce.26
  632.3 51.0 all-gather.24
  685.3 50.8 all-gather.20
  776.4 563.6 all-reduce.36
  1360.6 154.4 all-gather.26
  1604.7 127.5 all-reduce.28
  1752.9 50.1 all-gather.28
  1834.2 91.1 all-reduce.30
  1926.8 153.9 all-gather.22
  2086.5 126.1 all-gather.30
  2254.4 153.3 all-reduce.34
  2410.3 235.4 all-reduce.32
where the time goes:
time: 2750 us; the launch traced here: 2730 us
  waiting for transfers between devices  1820 us (66%)
  local copies, waits for them, and re-layouts  380 us (14%)
  matrix products  247 us (9%)
  other arithmetic  157 us (6%)
  blocking collectives  113 us (4%)
    unnamed x21, waiting for transfers between devices  1370 us
    all_gather x4, waiting for transfers between devices, halves_then_heads(): gathered = lax.all_gather(local_rows, 'col', axis=0, tiled=True)  222 us
    unnamed x93, local copies, waits for them, and re-layouts  149 us
    all_gather x4, waiting for transfers between devices, rows_then_width(): gathered = lax.all_gather(local_rows, 'row', axis=0, tiled=True)  148 us
    all_gather x4, local copies, waits for them, and re-layouts, halves_then_heads(): gathered = lax.all_gather(local_rows, 'col', axis=0, tiled=True)  117 us
    psum x1, waiting for transfers between devices, grid_body(): lax.psum(qkv_w_grad.astype(jnp.bfloat16), 'dp').astype(jnp.float32)  80.7 us
    psum x1, blocking collectives, grid_body(): lax.psum((first_gain_part, first_shift_part, second_gain_part, second_shi...  58.9 us
  transfers between devices with their start and end apart: 15, of which 14 were waited for; matrix products, arithmetic and copies ran while one was open for 14% of the time, Pallas kernels for 0%

commit v1 on v0

--- a/solution.py
+++ b/solution.py
@@ -7,6 +7,28 @@
 S = 729
 IMG_DEV = 8
 EPSILON = 1e-06
+
+
+def in_order(blocks, dim):
+    shape = list(blocks.shape[1:])
+    shape[dim] *= blocks.shape[0]
+    return jnp.moveaxis(blocks, 0, dim).reshape(shape)
+
+
+def collected_by_bits(x, axis):
+    size = lax.axis_size(axis)
+    blocks = x[None]
+    for level in range(size.bit_length() - 1):
+        bit = 1 << level
+        other = lax.ppermute(blocks, axis, [(i, i ^ bit) for i in range(size)])
+        both = jnp.stack([blocks, other])
+        upper = lax.axis_index(axis) >> level & 1
+        blocks = jnp.where(upper == 0, both, both[::-1]).reshape(-1, *x.shape)
+    return blocks
+
+
+def gather_by_bits(x, axis, dim):
+    return in_order(collected_by_bits(x, axis), dim)
 
 
 def gelu_tanh(tensor):
@@ -58,7 +80,7 @@
 
 
 def rows_then_width(local_rows, weight_fn):
-    gathered = lax.all_gather(local_rows, "row", axis=0, tiled=True)
+    gathered = gather_by_bits(local_rows, "row", 0)
     return (
         gathered,
         lax.psum_scatter(

time: 2750 us -> 2980 us (1.084)
  local copies, waits for them, and re-layouts: 380 us -> 473 us
  waiting for transfers between devices: 1820 us -> 1910 us
  other arithmetic: 157 us -> 200 us
    ppermute x0 -> x8, waiting for transfers between devices: none -> 174 us  [collected_by_bits(): other = lax.ppermute(blocks, axis, [(i, i ^ bit) for i in range(size)])]
    all_gather x4 -> x0, waiting for transfers between devices: 148 us -> none  [rows_then_width(): gathered = lax.all_gather(local_rows, 'row', axis=0, tiled=True)]
    select_n x0 -> x4, local copies, waits for them, and re-layouts: none -> 137 us  [collected_by_bits(): blocks = jnp.where(upper == 0, both, both[::-1]).reshape(-1, *x.shape)]
    unnamed x21 -> x17, waiting for transfers between devices: 1370 us -> 1420 us
    another operation x4 -> x8, local copies, waits for them, and re-layouts: 5.36 us -> 55.7 us  [the longest x4 50.3 us: in_order(): return jnp.moveaxis(blocks, 0, dim).reshape(shape)]
    unnamed x93 -> x97, local copies, waits for them, and re-layouts: 149 us -> 100 us
    all_gather x4 -> x0, local copies, waits for them, and re-layouts: 45.9 us -> none  [rows_then_width(): gathered = lax.all_gather(local_rows, 'row', axis=0, tiled=True)]
    another operation x0 -> x16, other arithmetic: none -> 38.9 us  [collected_by_bits(): both = jnp.stack([blocks, other])]
  transfers between devices with their start and end apart: 15 -> 19, of which waited for: 14 -> 17; matrix products, arithmetic and copies ran while one was open for 14% -> 14% of each run, Pallas kernels for 0% -> 0%
where the time goes in v1:
time: 2980 us; the launch traced here: 2960 us
  waiting for transfers between devices  1910 us (64%)
  local copies, waits for them, and re-layouts  473 us (16%)
  matrix products  248 us (8%)
  other arithmetic  200 us (7%)
  blocking collectives  113 us (4%)
    unnamed x17, waiting for transfers between devices  1420 us
    all_gather x4, waiting for transfers between devices, halves_then_heads(): gathered = lax.all_gather(local_rows, 'col', axis=0, tiled=True)  222 us
    ppermute x8, waiting for transfers between devices, collected_by_bits(): other = lax.ppermute(blocks, axis, [(i, i ^ bit) for i in range(size)])  174 us
    select_n x4, local copies, waits for them, and re-layouts, collected_by_bits(): blocks = jnp.where(upper == 0, both, both[::-1]).reshape(-1, *x.shape)  137 us
    all_gather x4, local copies, waits for them, and re-layouts, halves_then_heads(): gathered = lax.all_gather(local_rows, 'col', axis=0, tiled=True)  117 us
    unnamed x97, local copies, waits for them, and re-layouts  100 us
    psum x1, waiting for transfers between devices, grid_body(): lax.psum(qkv_w_grad.astype(jnp.bfloat16), 'dp').astype(jnp.float32)  88.2 us
  transfers between devices with their start and end apart: 19, of which 17 were waited for; matrix products, arithmetic and copies ran while one was open for 14% of the time, Pallas kernels for 0%

profile of v1, /device:TPU:0, one launch (start us, length us, event | category | flops | bytes accessed | tf_op | source)
XLA Modules:
  0.0 2962.0 jit_solution(17905666345566759515)
XLA Ops:
  9.9 9.6 all-reduce.12
  32.8 77.4 %collective-permute-done.1 = bf16[2,1458,576]{1,2,0:T(8,128)(2,1)} collective-permute-done((bf16[2,1458,576]{1,2,0:T(8,128)(2,1)}, bf16[2,1458,576]{1,2,0:T(8,128)(2,1)}, u32[]{:S(2)}, u32[]{:S(2)}) %collective-permute-start.1) | collective-permute-done | bytes 3359264 | tf_op jit(solution)/shard_map/ppermute | solution.py:23
  118.2 34.2 %copy.73 = bf16[2,2,1458,576]{2,1,0,3:T(2,128)(2,1)} copy(bf16[2,2,1458,576]{2,3,1,0:T(8,128)(2,1)} %reverse_select_fusion.3) | data formatting | bytes 13436928 | tf_op jit(solution)/shard_map/jit(_where)/select_n | solution.py:26
  152.3 12.6 reshape_reshape.12
  165.0 13.2 convolution_convert_fusion.2
  180.2 234.9 %all-reduce.25.cloned.1.call-done = bf16[5832,864]{0,1:T(8,128)(2,1)} async-done(((bf16[5832,864]{0,1:T(8,128)(2,1)}), bf16[5832,864]{0,1:T(8,128)(2,1)}) %all-reduce.25.cloned.1.call-update) | async-done | bytes 10077712
  451.0 32.2 %while.26 = (s32[]{:T(128)}, bf16[4,729,4,72]{1,3,2,0:T(8,128)(2,1)}, f32[4,4,729,1]{2,1,3,0:T(4,128)}, bf16[4,729,4,72]{1,3,2,0:T(8,128)(2,1)}, bf16[4,729,4,72...) while((s32[]{:T(128)}, bf16[4,729,4,72]{1,3,2,0:T(8,128)(2,1)}, ...), condition=%wide.region_8.9_spmd, body=%wide.region_5.8_spmd.sunk | while | flops 629433152 | bytes 27374712 | solution.py:119
  487.9 15.4 reshape.137
  503.4 47.8 %all-gather.9.cloned.1.call-done = bf16[2,2916,288]{1,2,0:T(8,128)(2,1)} async-done(((bf16[1,2916,288]{1,2,0:T(8,128)(2,1)}), bf16[2,2916,288]{1,2,0:T(8,128)(2,1)}) %all-gather.9.cloned.1.call-update) | async-done | bytes 3359248 | tf_op jit(solution)/shard_map/all_gather | solution.py:93
  564.0 8.5 convolution_convert_fusion.6
  588.4 176.8 %all-reduce.27.cloned.1.call-done = bf16[5832,576]{0,1:T(8,128)(2,1)} async-done(((bf16[5832,576]{0,1:T(8,128)(2,1)}), bf16[5832,576]{0,1:T(8,128)(2,1)}) %all-reduce.27.cloned.1.call-update) | async-done | bytes 6718480
  798.4 34.6 %copy.83 = bf16[2,2,1458,576]{2,1,0,3:T(2,128)(2,1)} copy(bf16[2,2,1458,576]{2,3,1,0:T(8,128)(2,1)} %get-tuple-element.213) | data formatting | bytes 13436928 | tf_op jit(solution)/shard_map/jit(_where)/select_n | solution.py:26
  833.0 12.6 reshape_reshape.14
  845.6 16.0 convolution_convert_fusion
  875.5 34.2 %copy.80 = bf16[2,2,1458,576]{2,1,0,3:T(2,128)(2,1)} copy(bf16[2,2,1458,576]{2,3,1,0:T(8,128)(2,1)} %reverse_select_fusion.2) | data formatting | bytes 13436928 | tf_op jit(solution)/shard_map/jit(_where)/select_n | solution.py:26
  909.6 12.5 reshape_reshape.13
  922.2 16.1 convolution_convert_fusion.1
  938.4 562.9 %all-reduce.37.cloned.1.call-done = (bf16[5832,1076]{0,1:T(8,128)(2,1)}, bf16[5832,1076]{0,1:T(8,128)(2,1)}) async-done(((bf16[5832,1076]{0,1:T(8,128)(2,1)}, bf16[5832,1076]{0,1:T(8,128)(2,1)}), (bf16[5832,1076]{0,1:T(8,128)(2,1)}, bf16[5832,1076]{0,1:T(8,128)(2,1)})) %all-reduce.37.cloned.1.call-update) | async-done | bytes 25100944
  1501.3 20.4 fusion.71
  1521.7 154.6 %all-gather.13.cloned.1.call-done = bf16[2,2916,1076]{1,2,0:T(8,128)(2,1)} async-done(((bf16[1,2916,1076]{1,2,0:T(8,128)(2,1)}), bf16[2,2916,1076]{1,2,0:T(8,128)(2,1)}) %all-gather.13.cloned.1.call-update) | async-done | bytes 12550480 | tf_op jit(solution)/shard_map/all_gather | solution.py:93
  1676.3 48.5 %copy.84 = bf16[2,2916,1076]{1,0,2:T(2,128)(2,1)} copy(bf16[2,2916,1076]{1,2,0:T(8,128)(2,1)} %all-gather.13.cloned.1.call-done) | data formatting | bytes 25100928 | tf_op jit(solution)/shard_map/all_gather | solution.py:93
  1724.9 25.6 reshape.142
  1750.5 15.3 convolution_convert_fusion.3
  1765.8 127.7 %all-reduce.29.cloned.1.call-done = bf16[5832,576]{0,1:T(8,128)(2,1)} async-done(((bf16[5832,576]{0,1:T(8,128)(2,1)}), bf16[5832,576]{0,1:T(8,128)(2,1)}) %all-reduce.29.cloned.1.call-update) | async-done | bytes 6718480
  1899.1 8.4 all-reduce.10
  1919.1 77.8 %collective-permute-done.7 = bf16[2,1458,576]{1,2,0:T(8,128)(2,1)S(1)} collective-permute-done((bf16[2,1458,576]{1,2,0:T(8,128)(2,1)S(1)}, bf16[2,1458,576]{1,2,0:T(8,128)(2,1)S(1)}, u32[]{:S(2)}, u32[]{:S(2)}) %collective-permute-start.7) | collective-permute-done | bytes 3359264 | tf_op jit(solution)/shard_map/ppermute | solution.py:23
  2006.9 34.2 %copy.86 = bf16[2,2,1458,576]{2,1,0,3:T(2,128)(2,1)} copy(bf16[2,2,1458,576]{2,3,1,0:T(8,128)(2,1)} %get-tuple-element.215) | data formatting | bytes 13436928 | tf_op jit(solution)/shard_map/jit(_where)/select_n | solution.py:26
  2041.1 12.6 reshape_reshape.15
  2061.7 89.7 %all-reduce.31.cloned.1.call-done = bf16[5832,288]{0,1:T(8,128)(2,1)} async-done(((bf16[5832,288]{0,1:T(8,128)(2,1)}), bf16[5832,288]{0,1:T(8,128)(2,1)}) %all-reduce.31.cloned.1.call-update) | async-done | bytes 3359248
  2164.8 121.4 %while.27 = (s32[]{:T(128)}, bf16[4,729,4,72]{1,3,2,0:T(8,128)(2,1)}, bf16[4,729,4,72]{1,3,2,0:T(8,128)(2,1)}, bf16[4,729,4,72]{1,3,2,0:T(8,128)(2,1)}, bf16[4,7...) while((s32[]{:T(128)}, ...), condition=%wide.region_25.26_spmd, body=%wide.region_23.25_spmd.sunk | while | flops 1557106048 | bytes 127373888 | solution.py:154
  2178.2 10.2 multiply_convert_fusion.9
  2208.3 10.2 multiply_convert_fusion.9
  2238.5 10.2 multiply_convert_fusion.9
  2268.7 10.2 multiply_convert_fusion.9
  2312.8 48.3 %copy.81 = bf16[2,2916,1076]{1,0,2:T(2,128)(2,1)} copy(bf16[2,2916,1076]{1,2,0:T(8,128)(2,1)} %all-gather.11.cloned.1.call-done) | data formatting | bytes 25100928 | tf_op jit(solution)/shard_map/all_gather | solution.py:93
  2361.1 25.6 reshape.140
  2386.7 14.6 fusion.89
  2401.4 14.8 fusion.88
  2419.8 19.2 all-gather.15.cloned.1.call-done
  2439.0 13.6 copy.94
  2452.6 14.2 reshape.144
  2466.8 12.3 multiply_convert_fusion.2
  2480.6 15.6 convolution_convert_fusion.4
  2496.2 12.3 convolution_convert_fusion.5
  2522.8 20.2 all-reduce.14
  2545.9 88.2 %all-reduce.35.cloned.1.call-done = (bf16[3,576,288]{1,2,0:T(8,128)(2,1)}, bf16[288,576]{1,0:T(8,128)(2,1)}, bf16[576,1076]{1,0:T(8,128)(2,1)}, bf16[1076,576]{0,1:T(8,128)(2,1)}) async-done(((bf16[3,576,288]{1,2,0:T(8,128)(2,1)}, bf16[288,576]{1,0:T(8,128)(2,1)}, bf16[576,1076]{1,0:T(8,128)(2,1)}, bf16[1076,576]{0,1:T(8,128)(2,1)}), (bf16[3,576,288]{1,2,0:T(8,128)(2,1)}, bf16[288,576]{1,0:T(8,128)(2,1)}, ...) | async-done | bytes 3806224 | tf_op jit(solution)/shard_map/psum | solution.py:244
  2642.4 229.9 %all-reduce.33.cloned.1.call-done = (bf16[5832,576]{0,1:T(8,128)(2,1)}, bf16[5832,576]{0,1:T(8,128)(2,1)}) async-done(((bf16[5832,576]{0,1:T(8,128)(2,1)}, bf16[5832,576]{0,1:T(8,128)(2,1)}), (bf16[5832,576]{0,1:T(8,128)(2,1)}, bf16[5832,576]{0,1:T(8,128)(2,1)})) %all-reduce.33.cloned.1.call-update) | async-done | bytes 13436944
  2896.6 58.4 %all-reduce.8 = (f32[576]{0:T(1024)}, f32[576]{0:T(1024)}, f32[576]{0:T(1024)}, f32[576]{0:T(1024)}) all-reduce(f32[576]{0:T(1024)S(1)} %broadcast_multiply_fusion.9, f32[576]{0:T(1024)S(1)} %broadcast_multiply_fusion.8, f32[576]{0:T(1024)S(1)} %get-tuple-element.242, ...), channel_id=1, replica_groups=mesh['dp'=4,'row'=4,'col'=2] {'dp','row'}, use_global_device_ids=true, to_apply=%region_40.41 | all-reduce | flops 2304 | bytes 18432 | tf_op jit(solution)/shard_map/psum | solution.py:257
  (281 shorter events, 383.7 us)
Async XLA Ops:
  7.2 915.0 %copy-start = (bf16[576,1076]{1,0:T(8,128)(2,1)S(1)}, bf16[576,1076]{1,0:T(8,128)(2,1)}, u32[]{:S(2)}) copy-start(bf16[576,1076]{1,0:T(8,128)(2,1)} %param.29) | copy-start | bytes 3718660
  7.2 12.3 copy-start.24
  7.2 12.3 copy-start.30
  7.2 407.9 %all-reduce.25.cloned.1.call-start = ((), (), s32[]{:S(2)}) async-start(), calls=%async_computation.4 | async-start | bytes 20348928
  19.5 6.4 copy-start.19
  19.5 6.4 copy-start.21
  23.3 3.9 collective-permute-start
  31.4 78.9 %collective-permute-start.1 = (bf16[2,1458,576]{1,2,0:T(8,128)(2,1)}, bf16[2,1458,576]{1,2,0:T(8,128)(2,1)}, u32[]{:S(2)}, u32[]{:S(2)}) collective-permute-start(bf16[2,1458,576]{1,2,0:T(8,128)(2,1)} %get-tuple-element.236), channel_id=1, source_target_pairs={{0,4},{2,6},{4,0},{6,2},{1,5},{3,7},{5,1},{7,3},{8,12},{10,14},{12... | collective-permute-start | bytes 10077704 | tf_op jit(solution)/shard_map/ppermute | solution.py:23
  152.3 12.6 copy-start.39
  178.2 373.0 %all-gather.9.cloned.1.call-start = ((), (), s32[]{:S(2)}) async-start(), calls=%async_computation | async-start | bytes 5087232 | tf_op jit(solution)/shard_map/all_gather | solution.py:93
  483.2 20.2 copy-start.6
  503.4 261.8 %all-reduce.27.cloned.1.call-start = ((), (), s32[]{:S(2)}) async-start(), calls=%async_computation.5 | async-start | bytes 13565952
  557.5 6.4 copy-start.41
  572.5 928.8 %all-reduce.37.cloned.1.call-start = ((), (), s32[]{:S(2)}) async-start(), calls=%async_computation.10 | async-start | bytes 50872320
  576.0 5.2 collective-permute-start.4
  583.0 182.1 %copy-start.33 = (f32[576]{0:T(1024)S(1)}, f32[576]{0:T(1024)}, u32[]{:S(2)}) copy-start(f32[576]{0:T(1024)} %param.24) | copy-start | bytes 6916
  586.9 192.1 %copy-start.23 = (f32[576]{0:T(1024)S(1)}, f32[576]{0:T(1024)}, u32[]{:S(2)}) copy-start(f32[576]{0:T(1024)} %param.27) | copy-start | bytes 6916
  586.9 192.1 %copy-start.31 = (f32[576]{0:T(1024)S(1)}, f32[576]{0:T(1024)}, u32[]{:S(2)}) copy-start(f32[576]{0:T(1024)} %param.28) | copy-start | bytes 6916
  586.9 203.3 %collective-permute-start.5 = (bf16[2,1458,576]{1,2,0:T(8,128)(2,1)}, bf16[2,1458,576]{1,2,0:T(8,128)(2,1)}, u32[]{:S(2)}, u32[]{:S(2)}) collective-permute-start(bf16[2,1458,576]{1,2,0:T(8,128)(2,1)} %get-tuple-element.230), channel_id=1, source_target_pairs={{0,4},{2,6},{4,0},{6,2},{1,5},{3,7},{5,1},{7,3},{8,12},{10,14},{12... | collective-permute-start | bytes 10077704 | tf_op jit(solution)/shard_map/ppermute | solution.py:23
  781.7 3.8 collective-permute-start.2
  789.7 78.9 %collective-permute-start.3 = (bf16[2,1458,576]{1,2,0:T(8,128)(2,1)}, bf16[2,1458,576]{1,2,0:T(8,128)(2,1)}, u32[]{:S(2)}, u32[]{:S(2)}) collective-permute-start(bf16[2,1458,576]{1,2,0:T(8,128)(2,1)} %get-tuple-element.234), channel_id=1, source_target_pairs={{0,4},{2,6},{4,0},{6,2},{1,5},{3,7},{5,1},{7,3},{8,12},{10,14},{12... | collective-permute-start | bytes 10077704 | tf_op jit(solution)/shard_map/ppermute | solution.py:23
  833.0 12.6 copy-start.37
  845.6 22.9 copy-start.12
  938.3 563.0 %copy-start.32 = (f32[1076]{0:T(1024)S(1)}, f32[1076]{0:T(1024)}, u32[]{:S(2)}) copy-start(f32[1076]{0:T(1024)} %param.30) | copy-start | bytes 12916
  938.3 738.0 %all-gather.13.cloned.1.call-start = ((), (), s32[]{:S(2)}) async-start(), calls=%async_computation.2 | async-start | bytes 19077120 | tf_op jit(solution)/shard_map/all_gather | solution.py:93
  1521.7 371.8 %all-reduce.29.cloned.1.call-start = ((), (), s32[]{:S(2)}) async-start(), calls=%async_computation.6 | async-start | bytes 13565952
  1765.8 385.6 %all-reduce.31.cloned.1.call-start = ((), (), s32[]{:S(2)}) async-start(), calls=%async_computation.7 | async-start | bytes 6782976
  1913.3 3.8 collective-permute-start.6
  1918.3 78.6 %collective-permute-start.7 = (bf16[2,1458,576]{1,2,0:T(8,128)(2,1)S(1)}, bf16[2,1458,576]{1,2,0:T(8,128)(2,1)S(1)}, u32[]{:S(2)}, u32[]{:S(2)}) collective-permute-start(bf16[2,1458,576]{1,2,0:T(8,128)(2,1)S(1)} %get-tuple-element.228), channel_id=1, source_target_pairs={{0,4},{2,6},{4,0},{6,2},{1,5},{3,7},{5,1},{7,3},{8,12},{10,14},{12... | collective-permute-start | bytes 10077704 | tf_op jit(solution)/shard_map/ppermute | solution.py:23
  2041.1 12.6 copy-start.42
  2060.7 252.0 %all-gather.11.cloned.1.call-start = ((), (), s32[]{:S(2)}) async-start(), calls=%async_computation.1 | async-start | bytes 19077120 | tf_op jit(solution)/shard_map/all_gather | solution.py:93
  2061.5 377.5 %all-gather.15.cloned.1.call-start = ((), (), s32[]{:S(2)}) async-start(), calls=%async_computation.3 | async-start | bytes 15261696 | tf_op jit(solution)/shard_map/all_gather | solution.py:93
  2292.0 8.6 copy-start.13
  2312.7 321.4 %all-reduce.35.cloned.1.call-start = ((), (), s32[]{:S(2)}) async-start(), calls=%async_computation.9 | async-start | bytes 8257536 | tf_op jit(solution)/shard_map/psum | solution.py:244
  2386.7 29.5 slice-start
  2401.4 14.8 slice-start.1
  2401.4 14.8 copy-start.16
  2480.6 15.7 copy-start.40
  2480.6 391.7 %all-reduce.33.cloned.1.call-start = ((), (), s32[]{:S(2)}) async-start(), calls=%async_computation.8 | async-start | bytes 27131904
  2509.2 6.5 copy-start.28
  2509.2 6.5 copy-start.29
  2509.2 6.5 copy-start.27
  2639.0 233.3 %copy-start.20 = (f32[1458]{0:T(1024)S(1)}, f32[1458]{0:T(1024)}, u32[]{:S(2)}) copy-start(f32[1458]{0:T(1024)} %copy-done.19) | copy-start | bytes 17500
  2639.0 233.3 %copy-start.22 = (f32[1458]{0:T(1024)S(1)}, f32[1458]{0:T(1024)}, u32[]{:S(2)}) copy-start(f32[1458]{0:T(1024)} %copy-done.21) | copy-start | bytes 17500
  2639.0 233.3 %copy-start.25 = (f32[576]{0:T(1024)S(1)}, f32[576]{0:T(1024)}, u32[]{:S(2)}) copy-start(f32[576]{0:T(1024)} %param.25) | copy-start | bytes 6916
  2642.4 243.3 %copy-start.34 = (f32[576]{0:T(1024)S(1)}, f32[576]{0:T(1024)}, u32[]{:S(2)}) copy-start(f32[576]{0:T(1024)} %param.32) | copy-start | bytes 6916
  2885.7 5.6 copy-start.4
  2885.7 69.2 %copy-start.1 = (bf16[576,1076]{1,0:T(8,128)(2,1)S(1)}, bf16[576,1076]{1,0:T(8,128)(2,1)}, u32[]{:S(2)}) copy-start(bf16[576,1076]{1,0:T(8,128)(2,1)} %param.29) | copy-start | bytes 3718660
  (27 other events, 89.3 us)
Sparse Core Ops, SparseCore 0:
  178.3 236.7 all-reduce.24
  503.5 47.6 all-gather.8
  572.6 192.5 all-reduce.26
  938.4 562.7 all-reduce.36
  1521.8 154.4 all-gather.12
  1765.9 127.5 all-reduce.28
  2060.9 90.4 all-reduce.30
  2152.9 153.9 all-gather.10
  2312.8 126.1 all-gather.14
  2480.7 153.3 all-reduce.34
  2636.7 235.4 all-reduce.32
